TPU v7x, 32 devices: a whole 2x2x4 slice. The times are simulated.
32 devices in a mesh: section: 4 (over x, core), seq: 8 (over z, y).
Axes of the slice: x: 2, y: 2, z: 4, core: 2. Of those that a mesh axis runs over, the one named last changes fastest.
Arguments:
- layer_input: bfloat16 [4, 512, 4, 1536], P('section', 'seq'), may hold values from -300 to 300
- norm_gain: float32 [4, 1536], P('section'), may hold values from 0.1 to 1.9
- queries: bfloat16 [4, 512, 4, 1024], P('section', 'seq'), may hold values from -6 to 6
- key_states: bfloat16 [4, 512, 4, 1024], P('section', 'seq'), may hold values from -6 to 6
- value_states: bfloat16 [4, 512, 4, 1024], P('section', 'seq'), may hold values from -6 to 6
- out_grad: bfloat16 [4, 512, 4, 1536], P('section', 'seq'), may hold values from -6 to 6
- out_weight: bfloat16 [4, 1024, 1536], P('section', 'seq'), may hold values from -0.1875 to 0.1875
- qkv_weight: bfloat16 [4, 1536, 3072], P('section', 'seq'), may hold values from -0.15625 to 0.15625
- lengths: int32 [4, 4], P('section'), may hold values from 256 to 512
Outputs:
- passed_grad: bfloat16 [4, 512, 4, 1536], P('section', 'seq')
All inputs are finite; a program needn't handle non-finite values.
Results may differ from a plain program's by a relative error of at most 0.0034.
Values may be sent and summed in bfloat16 or wider, within the bound.
A program may use at most 128 MiB of HBM per device.

v0:
```python
import jax
import jax.numpy as jnp
from jax import lax
from jax.sharding import PartitionSpec as P

HEADS = 16
HS = 64
EPSILON = 1e-05
MASKED = -1e30
ROW_DOT = (((1,), (1,)), ((), ()))
COL_DOT = (((0,), (0,)), ((), ()))


def shifted(shard, axis, by):
    count = lax.axis_size(axis)
    return lax.ppermute(shard, axis, [(i, (i + by) % count) for i in range(count)])


def item_backward(query_rows, key_rows, value_rows, grad_rows, key_valid):
    length = query_rows.shape[0]
    block = min(512, length)
    scale = HS ** (-0.5)
    offsets = jnp.arange(0, length, block)
    zeros = jnp.zeros((length, query_rows.shape[1]), jnp.float32)

    def step(carry, offset):
        key_total, value_total = carry
        query_block = lax.dynamic_slice_in_dim(query_rows, offset, block, 0)
        grad_block = lax.dynamic_slice_in_dim(grad_rows, offset, block, 0)
        scores = (
            lax.dot_general(query_block, key_rows, ROW_DOT, preferred_element_type=jnp.float32)
            * scale
        )
        scores = jnp.where(key_valid[None, :], scores, MASKED)
        largest = jnp.max(scores, axis=1, keepdims=True)
        weights = jnp.exp(scores - largest)
        probs = weights / jnp.sum(weights, axis=1, keepdims=True)
        probs_low = probs.astype(jnp.bfloat16)
        grad_probs = lax.dot_general(
            grad_block, value_rows, ROW_DOT, preferred_element_type=jnp.float32
        )
        centre = jnp.sum(probs * grad_probs, axis=1, keepdims=True)
        grad_scores = (probs * (grad_probs - centre) * scale).astype(jnp.bfloat16)
        query_grad = jnp.dot(grad_scores, key_rows, preferred_element_type=jnp.float32)
        key_total = key_total + lax.dot_general(
            grad_scores, query_block, COL_DOT, preferred_element_type=jnp.float32
        )
        value_total = value_total + lax.dot_general(
            probs_low, grad_block, COL_DOT, preferred_element_type=jnp.float32
        )
        return ((key_total, value_total), query_grad.astype(jnp.bfloat16))

    (key_total, value_total), query_parts = lax.scan(step, (zeros, zeros), offsets)
    query_grad = query_parts.reshape(length, query_rows.shape[1])
    return (query_grad, key_total.astype(jnp.bfloat16), value_total.astype(jnp.bfloat16))


def split_items(columns):
    length = columns.shape[0]
    count = columns.shape[1] // HS
    return columns.reshape(length, count, HS).transpose(1, 0, 2)


def join_items(items):
    count = items.shape[0]
    length = items.shape[1]
    return items.transpose(1, 0, 2).reshape(length, count * HS)


def project_grad(flat_grad, out_rows):
    return lax.dot_general(
        flat_grad,
        lax.all_gather(out_rows, "seq", axis=0, tiled=True),
        ROW_DOT,
        preferred_element_type=jnp.float32,
    ).astype(jnp.bfloat16)


def on_device(
    layer_input,
    norm_gain,
    queries,
    key_states,
    value_states,
    out_grad,
    out_weight,
    qkv_weight,
    lengths,
):
    frames = queries.shape[1]
    records = queries.shape[2]
    features = queries.shape[3]
    model_width = out_grad.shape[3]
    flat_grad = out_grad[0].reshape(frames * records, model_width)
    frame_queries = queries[0].reshape(frames, records * features)
    frame_keys = key_states[0].reshape(frames, records * features)
    frame_values = value_states[0].reshape(frames, records * features)
    attn_grad = project_grad(flat_grad, out_weight[0])
    head_queries, head_keys, head_values, head_grads = (
        lax.all_to_all(frame_queries, "seq", split_axis=1, concat_axis=0, tiled=True),
        lax.all_to_all(frame_keys, "seq", split_axis=1, concat_axis=0, tiled=True),
        lax.all_to_all(frame_values, "seq", split_axis=1, concat_axis=0, tiled=True),
        lax.all_to_all(
            attn_grad.reshape(frames, records * features),
            "seq",
            split_axis=1,
            concat_axis=0,
            tiled=True,
        ),
    )
    items_here = head_queries.shape[1] // HS
    length = head_queries.shape[0]
    item_ids = lax.axis_index("seq") * items_here + jnp.arange(items_here, dtype=jnp.int32)
    record_ids = item_ids // HEADS
    record_pick = jnp.arange(records, dtype=jnp.int32)[None, :] == record_ids[:, None]
    item_lengths = jnp.sum(jnp.where(record_pick, lengths[0][None, :], 0), axis=1)
    key_valid = jnp.arange(length, dtype=jnp.int32)[None, :] < item_lengths[:, None]
    query_grad, key_gradient, value_grad = lax.map(
        lambda group: item_backward(*group),
        (
            split_items(head_queries),
            split_items(head_keys),
            split_items(head_values),
            split_items(head_grads),
            key_valid,
        ),
    )
    query_back, key_backward, value_back = (
        lax.all_to_all(join_items(query_grad), "seq", split_axis=0, concat_axis=1, tiled=True),
        lax.all_to_all(join_items(key_gradient), "seq", split_axis=0, concat_axis=1, tiled=True),
        lax.all_to_all(join_items(value_grad), "seq", split_axis=0, concat_axis=1, tiled=True),
    )
    joined = jnp.concatenate(
        [
            query_back.reshape(frames * records, features),
            key_backward.reshape(frames * records, features),
            value_back.reshape(frames * records, features),
        ],
        axis=1,
    )
    norm_grad = lax.dot_general(
        joined,
        lax.all_gather(qkv_weight[0], "seq", axis=0, tiled=True),
        ROW_DOT,
        preferred_element_type=jnp.float32,
    )
    inputs = layer_input[0].reshape(frames * records, model_width).astype(jnp.float32)
    row_average = jnp.mean(inputs, axis=1, keepdims=True)
    centered_input = inputs - row_average
    var = jnp.mean(centered_input * centered_input, axis=1, keepdims=True)
    inverse_deviation = 1.0 / jnp.sqrt(var + EPSILON)
    normalized_input = centered_input * inverse_deviation
    scaled_rows = norm_grad * norm_gain[0][None, :]
    residual_branch = inverse_deviation * (
        scaled_rows
        - jnp.mean(scaled_rows, axis=1, keepdims=True)
        - normalized_input * jnp.mean(scaled_rows * normalized_input, axis=1, keepdims=True)
    )
    input_grad = (flat_grad.astype(jnp.float32) + residual_branch).astype(jnp.bfloat16)
    input_grad = input_grad.reshape(1, frames, records, model_width)
    return shifted(input_grad, "section", -1)


def solution(mesh):
    in_specs = (
        P("section", "seq", None, None),
        P("section", None),
        P("section", "seq", None, None),
        P("section", "seq", None, None),
        P("section", "seq", None, None),
        P("section", "seq", None, None),
        P("section", "seq", None),
        P("section", "seq", None),
        P("section", None),
    )
    out_specs = P("section", "seq", None, None)
    return jax.shard_map(
        on_device, mesh=mesh, in_specs=in_specs, out_specs=out_specs, check_vma=False
    )
```

profile of v0, /device:TPU:1, one launch (start us, length us, event | category | flops | bytes accessed | tf_op | source)
XLA Modules:
  0.0 301.7 jit_solution(11840325789857754773)
XLA Ops:
  7.3 1.2 all_to_all.84
  8.5 0.9 copy.24
  9.4 6.4 %all-to-all-start = ((bf16[64,8,512]{2,0,1:T(8,128)(2,1)}), bf16[64,8,512]{2,0,1:T(8,128)(2,1)S(1)}, u32[]{:S(2)}, u32[]{:S(2)}) async-start(bf16[64,8,512]{2,0,1:T(8,128)(2,1)} %copy.24), calls=%async_computation | async-start | bytes 1048576 | tf_op jit(solution)/shard_map/all_to_all | solution.py:100
  16.0 0.9 copy.25
  16.9 14.0 %all-to-all-done = bf16[64,8,512]{2,0,1:T(8,128)(2,1)S(1)} async-done(((bf16[64,8,512]{2,0,1:T(8,128)(2,1)}), bf16[64,8,512]{2,0,1:T(8,128)(2,1)S(1)}, u32[]{:S(2)}, u32[]{:S(2)}) %all-to-all-start) | async-done | bytes 524320 | tf_op jit(solution)/shard_map/all_to_all | solution.py:100
  31.0 13.1 %all-to-all-start.1 = ((bf16[64,8,512]{2,0,1:T(8,128)(2,1)}), bf16[64,8,512]{2,0,1:T(8,128)(2,1)S(1)}, u32[]{:S(2)}, u32[]{:S(2)}) async-start(bf16[64,8,512]{2,0,1:T(8,128)(2,1)} %copy.25), calls=%async_computation.1 | async-start | bytes 1048576 | tf_op jit(solution)/shard_map/all_to_all | solution.py:101
  44.2 0.9 copy.27
  45.1 15.1 %all-to-all-done.1 = bf16[64,8,512]{2,0,1:T(8,128)(2,1)S(1)} async-done(((bf16[64,8,512]{2,0,1:T(8,128)(2,1)}), bf16[64,8,512]{2,0,1:T(8,128)(2,1)S(1)}, u32[]{:S(2)}, u32[]{:S(2)}) %all-to-all-start.1) | async-done | bytes 524320 | tf_op jit(solution)/shard_map/all_to_all | solution.py:101
  60.3 14.4 %all-to-all-start.3 = ((bf16[64,8,512]{2,0,1:T(8,128)(2,1)}), bf16[64,8,512]{2,0,1:T(8,128)(2,1)S(1)}, u32[]{:S(2)}, u32[]{:S(2)}) async-start(bf16[64,8,512]{2,0,1:T(8,128)(2,1)} %copy.27), calls=%async_computation.3 | async-start | bytes 1048576 | tf_op jit(solution)/shard_map/all_to_all | solution.py:102
  74.9 18.9 %all-gather.5.cloned.1.call-done = bf16[1,1024,1536]{2,1,0:T(8,128)(2,1)} async-done(((bf16[1,128,1536]{2,1,0:T(8,128)(2,1)}), bf16[1,1024,1536]{2,1,0:T(8,128)(2,1)}) %all-gather.5.cloned.1.call-update) | async-done | bytes 3145744 | tf_op jit(solution)/shard_map/all_gather | solution.py:73
  93.8 2.9 fusion.43
  96.9 1.0 copy.26
  97.9 4.1 %all-to-all-start.2 = ((bf16[64,8,512]{2,0,1:T(8,128)(2,1)}), bf16[64,8,512]{2,0,1:T(8,128)(2,1)}, u32[]{:S(2)}, u32[]{:S(2)}) async-start(bf16[64,8,512]{2,0,1:T(8,128)(2,1)} %copy.26), calls=%async_computation.2 | async-start | bytes 1048576 | tf_op jit(solution)/shard_map/all_to_all | solution.py:103
  103.7 1.6 reshape.134
  105.5 1.6 reshape.136
  107.1 1.1 copy.31
  108.3 7.5 %all-to-all-done.2 = bf16[64,8,512]{2,0,1:T(8,128)(2,1)} async-done(((bf16[64,8,512]{2,0,1:T(8,128)(2,1)}), bf16[64,8,512]{2,0,1:T(8,128)(2,1)}, u32[]{:S(2)}, u32[]{:S(2)}) %all-to-all-start.2) | async-done | bytes 524320 | tf_op jit(solution)/shard_map/all_to_all | solution.py:103
  115.8 1.6 reshape.135
  117.5 1.2 copy.30
  118.7 46.5 %while.14 = (s32[]{:T(128)}, bf16[8,512,64]{1,2,0:T(8,128)(2,1)}, bf16[8,512,64]{1,2,0:T(8,128)(2,1)}, bf16[8,512,64]{1,2,0:T(8,128)(2,1)}, pred[8,512]{1,0:T(8,...) while((s32[]{:T(128)}, bf16[8,512,64]{1,2,0:T(8,128)(2,1)}, ...), condition=%wide.region_7.8_spmd, body=%wide.region_3.7_spmd.sunk | while | flops 172587520 | bytes 10056297 | solution.py:118
  119.2 1.8 fusion.73
  121.1 1.3 multiply_reduce_fusion.4
  122.7 0.9 fusion.72
  125.0 1.8 fusion.73
  126.9 1.3 multiply_reduce_fusion.4
  128.4 0.9 fusion.72
  130.8 1.9 fusion.73
  132.7 1.3 multiply_reduce_fusion.4
  134.3 0.9 fusion.72
  136.6 1.9 fusion.73
  138.5 1.3 multiply_reduce_fusion.4
  140.1 0.9 fusion.72
  142.4 1.9 fusion.73
  144.3 1.3 multiply_reduce_fusion.4
  145.8 0.9 fusion.72
  146.8 0.9 fusion.71
  148.2 1.8 fusion.73
  150.1 1.3 multiply_reduce_fusion.4
  151.6 0.9 fusion.72
  154.0 1.8 fusion.73
  155.8 1.3 multiply_reduce_fusion.4
  157.4 0.9 fusion.72
  159.8 1.8 fusion.73
  161.6 1.4 multiply_reduce_fusion.4
  163.3 0.9 fusion.72
  164.3 0.9 fusion.71
  165.1 1.6 reshape.144
  166.8 1.5 copy.38
  168.3 4.4 %all-to-all-start.4 = ((bf16[8,64,512]{2,1,0:T(8,128)(2,1)}), bf16[8,64,512]{2,1,0:T(8,128)(2,1)S(1)}, u32[]{:S(2)}, u32[]{:S(2)}) async-start(bf16[8,64,512]{2,1,0:T(8,128)(2,1)} %copy.38), calls=%async_computation.4 | async-start | bytes 1048576 | tf_op jit(solution)/shard_map/all_to_all | solution.py:129
  173.3 1.5 copy.39
  174.9 25.2 %all-to-all-done.4 = bf16[8,64,512]{2,1,0:T(8,128)(2,1)S(1)} async-done(((bf16[8,64,512]{2,1,0:T(8,128)(2,1)}), bf16[8,64,512]{2,1,0:T(8,128)(2,1)S(1)}, u32[]{:S(2)}, u32[]{:S(2)}) %all-to-all-start.4) | async-done | bytes 524320 | tf_op jit(solution)/shard_map/all_to_all | solution.py:129
  200.1 6.2 %all-to-all-start.5 = ((bf16[8,64,512]{2,1,0:T(8,128)(2,1)}), bf16[8,64,512]{2,1,0:T(8,128)(2,1)S(1)}, u32[]{:S(2)}, u32[]{:S(2)}) async-start(bf16[8,64,512]{2,1,0:T(8,128)(2,1)} %copy.39), calls=%async_computation.5 | async-start | bytes 1048576 | tf_op jit(solution)/shard_map/all_to_all | solution.py:130
  206.8 1.5 copy.40
  208.4 24.6 %all-to-all-done.5 = bf16[8,64,512]{2,1,0:T(8,128)(2,1)S(1)} async-done(((bf16[8,64,512]{2,1,0:T(8,128)(2,1)}), bf16[8,64,512]{2,1,0:T(8,128)(2,1)S(1)}, u32[]{:S(2)}, u32[]{:S(2)}) %all-to-all-start.5) | async-done | bytes 524320 | tf_op jit(solution)/shard_map/all_to_all | solution.py:130
  232.9 6.7 %all-to-all-start.6 = ((bf16[8,64,512]{2,1,0:T(8,128)(2,1)}), bf16[8,64,512]{2,1,0:T(8,128)(2,1)}, u32[]{:S(2)}, u32[]{:S(2)}) async-start(bf16[8,64,512]{2,1,0:T(8,128)(2,1)} %copy.40), calls=%async_computation.6 | async-start | bytes 1048576 | tf_op jit(solution)/shard_map/all_to_all | solution.py:131
  241.4 1.0 reshape.137
  242.8 23.1 %all-to-all-done.6 = bf16[8,64,512]{2,1,0:T(8,128)(2,1)} async-done(((bf16[8,64,512]{2,1,0:T(8,128)(2,1)}), bf16[8,64,512]{2,1,0:T(8,128)(2,1)}, u32[]{:S(2)}, u32[]{:S(2)}) %all-to-all-start.6) | async-done | bytes 524320 | tf_op jit(solution)/shard_map/all_to_all | solution.py:131
  265.9 1.3 copy.37
  267.2 1.0 reshape.139
  268.2 6.5 %all-gather.7.cloned.1.call-done = bf16[1,1536,3072]{2,1,0:T(8,128)(2,1)} async-done(((bf16[1,192,3072]{2,1,0:T(8,128)(2,1)}), bf16[1,1536,3072]{2,1,0:T(8,128)(2,1)}) %all-gather.7.cloned.1.call-update) | async-done | bytes 9437200 | tf_op jit(solution)/shard_map/all_gather | solution.py:143
  274.7 6.7 %fusion.47 = (f32[256]{0:T(256)S(1)}, f32[256]{0:T(256)S(1)}, f32[256,1536]{1,0:T(8,128)S(1)}) fusion(f32[256]{0:T(256)S(1)} %sqrt.6, f32[256,1536]{1,0:T(8,128)S(1)} %reshape.141, f32[256]{0:T(256)S(1)} %div.47, f32[1536]{0:T(1024)S(1)} %reduce.3, bf16[1,1536,3072]{2,1,0:T(8,128)(2,1)} %all-gather.7.cloned.1.call-done, bf16[256,1024]{1,0:T(8,128)(2,1)} %reshape.139, ...), kind=kOutput, calls=%fused_computation.66 | convolution fusion | flops 2422996480 | bytes 14166016 | tf_op jit(solution)/shard_map/dot_general | solution.py:141
  282.3 0.9 collective-permute-start
  283.2 10.7 %collective-permute-done = bf16[1,64,4,1536]{3,2,1,0:T(4,128)(2,1)S(1)} collective-permute-done((bf16[1,64,4,1536]{3,2,1,0:T(4,128)(2,1)S(1)}, bf16[1,64,4,1536]{3,2,1,0:T(4,128)(2,1)S(1)}, u32[]{:S(2)}, u32[]{:S(2)}) %collective-permute-start) | collective-permute-done | bytes 786464 | tf_op jit(solution)/shard_map/ppermute | solution.py:16
  294.0 0.9 copy.59
  (98 shorter events, 19.0 us)
Async XLA Ops:
  6.5 87.3 %all-gather.5.cloned.1.call-start = ((), (), s32[]{:S(2)}) async-start(), calls=%async_computation.7 | async-start | bytes 3538944 | tf_op jit(solution)/shard_map/all_gather | solution.py:73
  7.3 8.6 %copy-start.8 = (bf16[1,64,4,1024]{3,2,1,0:T(4,128)(2,1)S(1)}, bf16[1,64,4,1024]{3,2,1,0:T(4,128)(2,1)}, u32[]{:S(2)}) copy-start(bf16[1,64,4,1024]{3,2,1,0:T(4,128)(2,1)} %param.14) | copy-start | bytes 1572868
  9.4 21.5 %all-to-all-start = ((bf16[64,8,512]{2,0,1:T(8,128)(2,1)}), bf16[64,8,512]{2,0,1:T(8,128)(2,1)S(1)}, u32[]{:S(2)}, u32[]{:S(2)}) async-start(bf16[64,8,512]{2,0,1:T(8,128)(2,1)} %copy.24), calls=%async_computation | async-start | bytes 1048576 | tf_op jit(solution)/shard_map/all_to_all | solution.py:100
  15.8 28.2 %copy-start.9 = (bf16[1,64,4,1024]{3,2,1,0:T(4,128)(2,1)S(1)}, bf16[1,64,4,1024]{3,2,1,0:T(4,128)(2,1)}, u32[]{:S(2)}) copy-start(bf16[1,64,4,1024]{3,2,1,0:T(4,128)(2,1)} %param.15) | copy-start | bytes 1572868
  31.0 29.3 %all-to-all-start.1 = ((bf16[64,8,512]{2,0,1:T(8,128)(2,1)}), bf16[64,8,512]{2,0,1:T(8,128)(2,1)S(1)}, u32[]{:S(2)}, u32[]{:S(2)}) async-start(bf16[64,8,512]{2,0,1:T(8,128)(2,1)} %copy.25), calls=%async_computation.1 | async-start | bytes 1048576 | tf_op jit(solution)/shard_map/all_to_all | solution.py:101
  44.0 30.7 %copy-start.5 = (bf16[1,64,4,1536]{3,2,1,0:T(4,128)(2,1)S(1)}, bf16[1,64,4,1536]{3,2,1,0:T(4,128)(2,1)}, u32[]{:S(2)}) copy-start(bf16[1,64,4,1536]{3,2,1,0:T(4,128)(2,1)} %param.16) | copy-start | bytes 2359300
  60.3 36.4 %copy-start.3 = (bf16[64,8,512]{2,0,1:T(8,128)(2,1)}, bf16[64,8,512]{2,0,1:T(8,128)(2,1)S(1)}, u32[]{:S(2)}) copy-start(bf16[64,8,512]{2,0,1:T(8,128)(2,1)S(1)} %all-to-all-done.1) | copy-start | bytes 1572868
  60.3 37.6 %all-to-all-start.3 = ((bf16[64,8,512]{2,0,1:T(8,128)(2,1)}), bf16[64,8,512]{2,0,1:T(8,128)(2,1)S(1)}, u32[]{:S(2)}, u32[]{:S(2)}) async-start(bf16[64,8,512]{2,0,1:T(8,128)(2,1)} %copy.27), calls=%async_computation.3 | async-start | bytes 1048576 | tf_op jit(solution)/shard_map/all_to_all | solution.py:102
  74.9 21.8 %copy-start.1 = (bf16[256,1536]{1,0:T(8,128)(2,1)}, bf16[256,1536]{1,0:T(8,128)(2,1)S(1)}, u32[]{:S(2)}) copy-start(bf16[256,1536]{1,0:T(8,128)(2,1)S(1)} %reshape_squeeze.2) | copy-start | bytes 2359300
  96.9 5.9 %copy-start.12 = (s32[1,4]{1,0:T(1,128)S(1)}, s32[1,4]{1,0:T(1,128)}, u32[]{:S(2)}) copy-start(s32[1,4]{1,0:T(1,128)} %param.19) | copy-start | bytes 52
  97.9 5.1 %copy-start.4 = (bf16[64,8,512]{2,0,1:T(8,128)(2,1)}, bf16[64,8,512]{2,0,1:T(8,128)(2,1)S(1)}, u32[]{:S(2)}) copy-start(bf16[64,8,512]{2,0,1:T(8,128)(2,1)S(1)} %all-to-all-done.3) | copy-start | bytes 1572868
  97.9 17.9 %all-to-all-start.2 = ((bf16[64,8,512]{2,0,1:T(8,128)(2,1)}), bf16[64,8,512]{2,0,1:T(8,128)(2,1)}, u32[]{:S(2)}, u32[]{:S(2)}) async-start(bf16[64,8,512]{2,0,1:T(8,128)(2,1)} %copy.26), calls=%async_computation.2 | async-start | bytes 1048576 | tf_op jit(solution)/shard_map/all_to_all | solution.py:103
  102.1 172.7 %all-gather.7.cloned.1.call-start = ((), (), s32[]{:S(2)}) async-start(), calls=%async_computation.8 | async-start | bytes 10616832 | tf_op jit(solution)/shard_map/all_gather | solution.py:143
  166.8 6.0 %copy-start.6 = (bf16[8,512,64]{1,2,0:T(8,128)(2,1)S(1)}, bf16[8,512,64]{1,2,0:T(8,128)(2,1)}, u32[]{:S(2)}) copy-start(bf16[8,512,64]{1,2,0:T(8,128)(2,1)} %get-tuple-element.82) | copy-start | bytes 1572868
  168.3 31.7 %all-to-all-start.4 = ((bf16[8,64,512]{2,1,0:T(8,128)(2,1)}), bf16[8,64,512]{2,1,0:T(8,128)(2,1)S(1)}, u32[]{:S(2)}, u32[]{:S(2)}) async-start(bf16[8,64,512]{2,1,0:T(8,128)(2,1)} %copy.38), calls=%async_computation.4 | async-start | bytes 1048576 | tf_op jit(solution)/shard_map/all_to_all | solution.py:129
  173.3 33.0 %copy-start.7 = (bf16[8,512,64]{1,2,0:T(8,128)(2,1)S(1)}, bf16[8,512,64]{1,2,0:T(8,128)(2,1)}, u32[]{:S(2)}) copy-start(bf16[8,512,64]{1,2,0:T(8,128)(2,1)} %get-tuple-element.83) | copy-start | bytes 1572868
  200.1 32.9 %all-to-all-start.5 = ((bf16[8,64,512]{2,1,0:T(8,128)(2,1)}), bf16[8,64,512]{2,1,0:T(8,128)(2,1)S(1)}, u32[]{:S(2)}, u32[]{:S(2)}) async-start(bf16[8,64,512]{2,1,0:T(8,128)(2,1)} %copy.39), calls=%async_computation.5 | async-start | bytes 1048576 | tf_op jit(solution)/shard_map/all_to_all | solution.py:130
  206.8 32.8 %copy-start = (bf16[1,64,4,1536]{3,2,1,0:T(4,128)(2,1)S(1)}, bf16[1,64,4,1536]{3,2,1,0:T(4,128)(2,1)}, u32[]{:S(2)}) copy-start(bf16[1,64,4,1536]{3,2,1,0:T(4,128)(2,1)} %param.11) | copy-start | bytes 2359300
  232.9 33.0 %all-to-all-start.6 = ((bf16[8,64,512]{2,1,0:T(8,128)(2,1)}), bf16[8,64,512]{2,1,0:T(8,128)(2,1)}, u32[]{:S(2)}, u32[]{:S(2)}) async-start(bf16[8,64,512]{2,1,0:T(8,128)(2,1)} %copy.40), calls=%async_computation.6 | async-start | bytes 1048576 | tf_op jit(solution)/shard_map/all_to_all | solution.py:131
  239.7 1.4 copy-start.11
  242.7 32.1 %copy-start.10 = (bf16[256,1024]{1,0:T(8,128)(2,1)S(1)}, bf16[256,1024]{1,0:T(8,128)(2,1)}, u32[]{:S(2)}) copy-start(bf16[256,1024]{1,0:T(8,128)(2,1)} %reshape.137) | copy-start | bytes 1572868
  268.2 13.3 %copy-start.2 = (bf16[256,1536]{1,0:T(8,128)(2,1)S(1)}, bf16[256,1536]{1,0:T(8,128)(2,1)}, u32[]{:S(2)}) copy-start(bf16[256,1536]{1,0:T(8,128)(2,1)} %copy-done.1) | copy-start | bytes 2359300
  282.3 11.6 %collective-permute-start = (bf16[1,64,4,1536]{3,2,1,0:T(4,128)(2,1)S(1)}, bf16[1,64,4,1536]{3,2,1,0:T(4,128)(2,1)S(1)}, u32[]{:S(2)}, u32[]{:S(2)}) collective-permute-start(bf16[1,64,4,1536]{3,2,1,0:T(4,128)(2,1)S(1)} %reshape.140), channel_id=1, source_target_pairs={{0,24},{8,0},{16,8},{24,16},{1,25},{9,1},{17,9},{25,17},{2,26},{10... | collective-permute-start | bytes 2359304 | tf_op jit(solution)/shard_map/ppermute | solution.py:16
Sparse Core Ops, SparseCore 0:
  9.5 84.2 all-gather.4
  105.0 169.6 all-gather.6
where the time goes:
time: 303 us; the launch traced here: 302 us
  waiting for transfers between devices  147 us (49%)
  starting transfers between devices  56.3 us (19%)
  matrix products  51.9 us (17%)
  local copies, waits for them, and re-layouts  26.7 us (9%)
  between operations  13.7 us (5%)
  other arithmetic  5.78 us (2%)
    all_to_all x1, waiting for transfers between devices, on_device(): lax.all_to_all(join_items(query_grad), 'seq', split_axis=0, concat_axis=1...  25.2 us
    all_to_all x1, waiting for transfers between devices, on_device(): lax.all_to_all(join_items(key_gradient), 'seq', split_axis=0, concat_axis...  24.6 us
    all_to_all x1, waiting for transfers between devices, on_device(): lax.all_to_all(join_items(value_grad), 'seq', split_axis=0, concat_axis=1...  23.1 us
    all_gather x1, waiting for transfers between devices, project_grad(): lax.all_gather(out_rows, 'seq', axis=0, tiled=True)  18.9 us
    all_to_all x1, waiting for transfers between devices, on_device(): lax.all_to_all(frame_keys, 'seq', split_axis=1, concat_axis=0, tiled=True)  15.1 us
    dot_general x8, matrix products, step(): lax.dot_general(probs_low, grad_block, COL_DOT, preferred_element_type=jn...  14.8 us
    all_to_all x1, starting transfers between devices, on_device(): lax.all_to_all(frame_values, 'seq', split_axis=1, concat_axis=0, tiled=True)  14.4 us
    all_to_all x1, waiting for transfers between devices, on_device(): lax.all_to_all(frame_queries, 'seq', split_axis=1, concat_axis=0, tiled=T...  14 us
  transfers between devices with their start and end apart: 10, of which 9 were waited for; matrix products, arithmetic and copies ran while one was open for 25% of the time, Pallas kernels for 0%

commit v1 on v0

--- a/solution.py
+++ b/solution.py
@@ -9,6 +9,28 @@
 MASKED = -1e30
 ROW_DOT = (((1,), (1,)), ((), ()))
 COL_DOT = (((0,), (0,)), ((), ()))
+
+
+def joined_along(blocks, dim):
+    shape = list(blocks.shape[1:])
+    shape[dim] *= blocks.shape[0]
+    return jnp.moveaxis(blocks, 0, dim).reshape(shape)
+
+
+def ring_gather(value, axis, dim):
+    peers = lax.axis_size(axis)
+    pairs = [(i, (i + 1) % peers) for i in range(peers)]
+    back = [(b, a) for a, b in pairs]
+    lower, upper = ([], [])
+    for step in range(peers - 1):
+        if step % 2 == 0:
+            lower.append(lax.ppermute(lower[-1] if lower else value, axis, pairs))
+        else:
+            upper.append(lax.ppermute(upper[-1] if upper else value, axis, back))
+    parts = jnp.stack([*lower[::-1], value, *upper])
+    shift = lax.axis_index(axis) - len(lower)
+    parts = parts[(jnp.arange(peers) - shift) % peers]
+    return joined_along(parts, dim)
 
 
 def shifted(shard, axis, by):
@@ -69,10 +91,7 @@
 
 def project_grad(flat_grad, out_rows):
     return lax.dot_general(
-        flat_grad,
-        lax.all_gather(out_rows, "seq", axis=0, tiled=True),
-        ROW_DOT,
-        preferred_element_type=jnp.float32,
+        flat_grad, ring_gather(out_rows, "seq", 0), ROW_DOT, preferred_element_type=jnp.float32
     ).astype(jnp.bfloat16)
 
 

time: 303 us -> 325 us (1.073)
  local copies, waits for them, and re-layouts: 26.7 us -> 39.6 us
  starting transfers between devices: 56.3 us -> 64.4 us
    ppermute x0 -> x7, waiting for transfers between devices: none -> 29.2 us  [the longest x4 29.2 us: ring_gather(): lower.append(lax.ppermute(lower[-1] if lower else value, axis, pairs))]
    ppermute x0 -> x7, starting transfers between devices: none -> 25.6 us  [the longest x3 19.1 us: ring_gather(): upper.append(lax.ppermute(upper[-1] if upper else value, axis, back))]
    all_gather x1 -> x0, waiting for transfers between devices: 18.9 us -> none  [project_grad(): lax.all_gather(out_rows, 'seq', axis=0, tiled=True)]
    all_to_all x1, waiting for transfers between devices: 14 us -> 0.81 us  [on_device(): lax.all_to_all(frame_queries, 'seq', split_axis=1, concat_axis=0, tiled=T...]
    all_to_all x1, starting transfers between devices: 14.4 us -> 4.16 us  [on_device(): lax.all_to_all(frame_values, 'seq', split_axis=1, concat_axis=0, tiled=True)]
    unnamed x27 -> x36, local copies, waits for them, and re-layouts: 0.95 us -> 7.11 us
    all_to_all x1, waiting for transfers between devices: 0.01 us -> 4.41 us  [on_device(): lax.all_to_all(frame_values, 'seq', split_axis=1, concat_axis=0, tiled=True)]
    all_to_all x1, waiting for transfers between devices: 15.1 us -> 11.3 us  [on_device(): lax.all_to_all(frame_keys, 'seq', split_axis=1, concat_axis=0, tiled=True)]
  transfers between devices with their start and end apart: 10 -> 16, of which waited for: 9 -> 12; matrix products, arithmetic and copies ran while one was open for 25% -> 27% of each run, Pallas kernels for 0% -> 0%
where the time goes in v1:
time: 325 us; the launch traced here: 323 us
  waiting for transfers between devices  148 us (46%)
  starting transfers between devices  64.4 us (20%)
  matrix products  52.1 us (16%)
  local copies, waits for them, and re-layouts  39.6 us (12%)
  between operations  13.8 us (4%)
  other arithmetic  5.8 us (2%)
    ppermute x4, waiting for transfers between devices, ring_gather(): lower.append(lax.ppermute(lower[-1] if lower else value, axis, pairs))  29.2 us
    all_to_all x1, waiting for transfers between devices, on_device(): lax.all_to_all(join_items(value_grad), 'seq', split_axis=0, concat_axis=1...  26.8 us
    all_to_all x1, waiting for transfers between devices, on_device(): lax.all_to_all(join_items(key_gradient), 'seq', split_axis=0, concat_axis...  26.3 us
    all_to_all x1, waiting for transfers between devices, on_device(): lax.all_to_all(join_items(query_grad), 'seq', split_axis=0, concat_axis=1...  24.7 us
    ppermute x3, starting transfers between devices, ring_gather(): upper.append(lax.ppermute(upper[-1] if upper else value, axis, back))  19.1 us
    dot_general x8, matrix products, step(): lax.dot_general(probs_low, grad_block, COL_DOT, preferred_element_type=jn...  14.9 us
    all_to_all x1, starting transfers between devices, on_device(): lax.all_to_all(frame_keys, 'seq', split_axis=1, concat_axis=0, tiled=True)  13.2 us
    all_to_all x1, waiting for transfers between devices, on_device(): lax.all_to_all(frame_keys, 'seq', split_axis=1, concat_axis=0, tiled=True)  11.3 us
  transfers between devices with their start and end apart: 16, of which 12 were waited for; matrix products, arithmetic and copies ran while one was open for 27% of the time, Pallas kernels for 0%

profile of v1, /device:TPU:1, one launch (start us, length us, event | category | flops | bytes accessed | tf_op | source)
XLA Modules:
  0.0 323.4 jit_solution(13432602310754747131)
XLA Ops:
  6.5 2.1 collective-permute-start
  8.6 12.1 %collective-permute-done = bf16[128,1536]{1,0:T(8,128)(2,1)S(1)} collective-permute-done((bf16[128,1536]{1,0:T(8,128)(2,1)}, bf16[128,1536]{1,0:T(8,128)(2,1)S(1)}, u32[]{:S(2)}, u32[]{:S(2)}) %collective-permute-start) | collective-permute-done | bytes 393248 | tf_op jit(solution)/shard_map/ppermute | solution.py:27
  20.7 4.2 %collective-permute-start.4 = (bf16[128,1536]{1,0:T(8,128)(2,1)}, bf16[128,1536]{1,0:T(8,128)(2,1)S(1)}, u32[]{:S(2)}, u32[]{:S(2)}) collective-permute-start(bf16[128,1536]{1,0:T(8,128)(2,1)} %bitcast.125), channel_id=1, source_target_pairs={{1,0},{2,1},{3,2},{4,3},{5,4},{6,5},{7,6},{0,7},{9,8},{10,9},{11,1... | collective-permute-start | bytes 1179656 | tf_op jit(solution)/shard_map/ppermute | solution.py:29
  24.8 11.8 %collective-permute-done.1 = bf16[128,1536]{1,0:T(8,128)(2,1)S(1)} collective-permute-done((bf16[128,1536]{1,0:T(8,128)(2,1)S(1)}, bf16[128,1536]{1,0:T(8,128)(2,1)S(1)}, u32[]{:S(2)}, u32[]{:S(2)}) %collective-permute-start.1) | collective-permute-done | bytes 393248 | tf_op jit(solution)/shard_map/ppermute | solution.py:27
  36.6 2.2 collective-permute-start.2
  38.8 10.9 %collective-permute-start.5 = (bf16[128,1536]{1,0:T(8,128)(2,1)S(1)}, bf16[128,1536]{1,0:T(8,128)(2,1)}, u32[]{:S(2)}, u32[]{:S(2)}) collective-permute-start(bf16[128,1536]{1,0:T(8,128)(2,1)S(1)} %collective-permute-done.4), channel_id=1, source_target_pairs={{1,0},{2,1},{3,2},{4,3},{5,4},{6,5},{7,6},{0,7},{9,8},{10,9},{11,1... | collective-permute-start | bytes 1179656 | tf_op jit(solution)/shard_map/ppermute | solution.py:29
  49.7 5.4 %collective-permute-done.2 = bf16[128,1536]{1,0:T(8,128)(2,1)S(1)} collective-permute-done((bf16[128,1536]{1,0:T(8,128)(2,1)S(1)}, bf16[128,1536]{1,0:T(8,128)(2,1)S(1)}, u32[]{:S(2)}, u32[]{:S(2)}) %collective-permute-start.2) | collective-permute-done | bytes 393248 | tf_op jit(solution)/shard_map/ppermute | solution.py:27
  55.0 2.2 collective-permute-start.3
  57.2 1.2 all_to_all.84
  59.4 4.2 %all-to-all-start = ((bf16[64,8,512]{2,0,1:T(8,128)(2,1)}), bf16[64,8,512]{2,0,1:T(8,128)(2,1)}, u32[]{:S(2)}, u32[]{:S(2)}) async-start(bf16[64,8,512]{2,0,1:T(8,128)(2,1)} %copy.40), calls=%async_computation | async-start | bytes 1048576 | tf_op jit(solution)/shard_map/all_to_all | solution.py:119
  63.6 1.1 reshape_squeeze.2
  66.8 4.1 %collective-permute-start.6 = (bf16[128,1536]{1,0:T(8,128)(2,1)}, bf16[128,1536]{1,0:T(8,128)(2,1)}, u32[]{:S(2)}, u32[]{:S(2)}) collective-permute-start(bf16[128,1536]{1,0:T(8,128)(2,1)} %collective-permute-done.5), channel_id=1, source_target_pairs={{1,0},{2,1},{3,2},{4,3},{5,4},{6,5},{7,6},{0,7},{9,8},{10,9},{11,1... | collective-permute-start | bytes 1179656 | tf_op jit(solution)/shard_map/ppermute | solution.py:29
  71.0 1.0 bitcast_dynamic-update-slice_fusion.6
  72.0 1.0 bitcast_dynamic-update-slice_fusion.5
  73.0 1.0 bitcast_dynamic-update-slice_fusion.4
  74.8 13.2 %all-to-all-start.1 = ((bf16[64,8,512]{2,0,1:T(8,128)(2,1)}), bf16[64,8,512]{2,0,1:T(8,128)(2,1)}, u32[]{:S(2)}, u32[]{:S(2)}) async-start(bf16[64,8,512]{2,0,1:T(8,128)(2,1)} %copy.41), calls=%async_computation.1 | async-start | bytes 1048576 | tf_op jit(solution)/shard_map/all_to_all | solution.py:120
  89.1 1.0 bitcast_dynamic-update-slice_fusion.2
  90.2 11.3 %all-to-all-done.1 = bf16[64,8,512]{2,0,1:T(8,128)(2,1)} async-done(((bf16[64,8,512]{2,0,1:T(8,128)(2,1)}), bf16[64,8,512]{2,0,1:T(8,128)(2,1)}, u32[]{:S(2)}, u32[]{:S(2)}) %all-to-all-start.1) | async-done | bytes 524320 | tf_op jit(solution)/shard_map/all_to_all | solution.py:120
  101.5 4.2 %all-to-all-start.3 = ((bf16[64,8,512]{2,0,1:T(8,128)(2,1)}), bf16[64,8,512]{2,0,1:T(8,128)(2,1)}, u32[]{:S(2)}, u32[]{:S(2)}) async-start(bf16[64,8,512]{2,0,1:T(8,128)(2,1)} %copy.44), calls=%async_computation.3 | async-start | bytes 1048576 | tf_op jit(solution)/shard_map/all_to_all | solution.py:121
  105.6 1.0 bitcast_dynamic-update-slice_fusion.1
  106.7 1.0 bitcast_dynamic-update-slice_fusion
  107.7 2.4 gather_fusion
  110.1 3.1 fusion.41
  114.5 4.4 %all-to-all-done.3 = bf16[64,8,512]{2,0,1:T(8,128)(2,1)} async-done(((bf16[64,8,512]{2,0,1:T(8,128)(2,1)}), bf16[64,8,512]{2,0,1:T(8,128)(2,1)}, u32[]{:S(2)}, u32[]{:S(2)}) %all-to-all-start.3) | async-done | bytes 524320 | tf_op jit(solution)/shard_map/all_to_all | solution.py:121
  118.9 4.2 %all-to-all-start.2 = ((bf16[64,8,512]{2,0,1:T(8,128)(2,1)}), bf16[64,8,512]{2,0,1:T(8,128)(2,1)}, u32[]{:S(2)}, u32[]{:S(2)}) async-start(bf16[64,8,512]{2,0,1:T(8,128)(2,1)} %copy.43), calls=%async_computation.2 | async-start | bytes 1048576 | tf_op jit(solution)/shard_map/all_to_all | solution.py:122
  124.1 1.6 reshape.185
  125.9 1.6 reshape.186
  127.7 1.6 reshape.189
  129.3 1.1 copy.48
  130.5 6.0 %all-to-all-done.2 = bf16[64,8,512]{2,0,1:T(8,128)(2,1)} async-done(((bf16[64,8,512]{2,0,1:T(8,128)(2,1)}), bf16[64,8,512]{2,0,1:T(8,128)(2,1)}, u32[]{:S(2)}, u32[]{:S(2)}) %all-to-all-start.2) | async-done | bytes 524320 | tf_op jit(solution)/shard_map/all_to_all | solution.py:122
  136.5 1.7 reshape.188
  138.2 1.2 copy.47
  139.3 46.5 %while.14 = (s32[]{:T(128)}, bf16[8,512,64]{1,2,0:T(8,128)(2,1)}, bf16[8,512,64]{1,2,0:T(8,128)(2,1)}, bf16[8,512,64]{1,2,0:T(8,128)(2,1)}, pred[8,512]{1,0:T(8,...) while((s32[]{:T(128)}, bf16[8,512,64]{1,2,0:T(8,128)(2,1)}, ...), condition=%wide.region_7.8_spmd, body=%wide.region_3.7_spmd.sunk | while | flops 172587520 | bytes 10056297 | solution.py:137
  139.9 1.9 fusion.72
  141.7 1.3 multiply_reduce_fusion.4
  145.7 1.9 fusion.72
  147.5 1.3 multiply_reduce_fusion.4
  151.5 1.9 fusion.72
  153.3 1.3 multiply_reduce_fusion.4
  157.3 1.9 fusion.72
  159.2 1.3 multiply_reduce_fusion.4
  163.1 1.9 fusion.72
  165.0 1.3 multiply_reduce_fusion.4
  168.9 1.9 fusion.72
  170.8 1.3 multiply_reduce_fusion.4
  174.8 1.9 fusion.72
  176.6 1.3 multiply_reduce_fusion.4
  180.6 1.9 fusion.72
  182.4 1.3 multiply_reduce_fusion.4
  185.8 1.7 reshape.204
  187.5 1.5 copy.55
  189.1 4.3 %all-to-all-start.4 = ((bf16[8,64,512]{2,1,0:T(8,128)(2,1)}), bf16[8,64,512]{2,1,0:T(8,128)(2,1)S(1)}, u32[]{:S(2)}, u32[]{:S(2)}) async-start(bf16[8,64,512]{2,1,0:T(8,128)(2,1)} %copy.55), calls=%async_computation.4 | async-start | bytes 1048576 | tf_op jit(solution)/shard_map/all_to_all | solution.py:148
  193.9 1.5 copy.56
  195.4 24.7 %all-to-all-done.4 = bf16[8,64,512]{2,1,0:T(8,128)(2,1)S(1)} async-done(((bf16[8,64,512]{2,1,0:T(8,128)(2,1)}), bf16[8,64,512]{2,1,0:T(8,128)(2,1)S(1)}, u32[]{:S(2)}, u32[]{:S(2)}) %all-to-all-start.4) | async-done | bytes 524320 | tf_op jit(solution)/shard_map/all_to_all | solution.py:148
  220.2 3.7 %all-to-all-start.5 = ((bf16[8,64,512]{2,1,0:T(8,128)(2,1)}), bf16[8,64,512]{2,1,0:T(8,128)(2,1)S(1)}, u32[]{:S(2)}, u32[]{:S(2)}) async-start(bf16[8,64,512]{2,1,0:T(8,128)(2,1)} %copy.56), calls=%async_computation.5 | async-start | bytes 1048576 | tf_op jit(solution)/shard_map/all_to_all | solution.py:149
  223.8 1.6 reshape.206
  225.5 1.5 copy.57
  227.0 26.3 %all-to-all-done.5 = bf16[8,64,512]{2,1,0:T(8,128)(2,1)S(1)} async-done(((bf16[8,64,512]{2,1,0:T(8,128)(2,1)}), bf16[8,64,512]{2,1,0:T(8,128)(2,1)S(1)}, u32[]{:S(2)}, u32[]{:S(2)}) %all-to-all-start.5) | async-done | bytes 524320 | tf_op jit(solution)/shard_map/all_to_all | solution.py:149
  253.3 4.2 %all-to-all-start.6 = ((bf16[8,64,512]{2,1,0:T(8,128)(2,1)}), bf16[8,64,512]{2,1,0:T(8,128)(2,1)}, u32[]{:S(2)}, u32[]{:S(2)}) async-start(bf16[8,64,512]{2,1,0:T(8,128)(2,1)} %copy.57), calls=%async_computation.6 | async-start | bytes 1048576 | tf_op jit(solution)/shard_map/all_to_all | solution.py:150
  260.7 26.8 %all-to-all-done.6 = bf16[8,64,512]{2,1,0:T(8,128)(2,1)} async-done(((bf16[8,64,512]{2,1,0:T(8,128)(2,1)}), bf16[8,64,512]{2,1,0:T(8,128)(2,1)}, u32[]{:S(2)}, u32[]{:S(2)}) %all-to-all-start.6) | async-done | bytes 524320 | tf_op jit(solution)/shard_map/all_to_all | solution.py:150
  287.4 1.3 copy.54
  289.7 6.8 %all-gather.3.cloned.1.call-done = bf16[1,1536,3072]{2,1,0:T(8,128)(2,1)} async-done(((bf16[1,192,3072]{2,1,0:T(8,128)(2,1)}), bf16[1,1536,3072]{2,1,0:T(8,128)(2,1)}) %all-gather.3.cloned.1.call-update) | async-done | bytes 9437200 | tf_op jit(solution)/shard_map/all_gather | solution.py:162
  296.5 6.7 %fusion.45 = (f32[256]{0:T(256)S(1)}, f32[256]{0:T(256)S(1)}, f32[256,1536]{1,0:T(8,128)S(1)}) fusion(f32[256]{0:T(256)S(1)} %sqrt.6, f32[256,1536]{1,0:T(8,128)S(1)} %reshape.194, f32[256]{0:T(256)S(1)} %div.47, f32[1536]{0:T(1024)S(1)} %reduce.3, bf16[1,1536,3072]{2,1,0:T(8,128)(2,1)} %all-gather.3.cloned.1.call-done, bf16[256,1024]{1,0:T(8,128)(2,1)} %reshape.192, ...), kind=kOutput, calls=%fused_computation.81 | convolution fusion | flops 2422996480 | bytes 14166016 | tf_op jit(solution)/shard_map/dot_general | solution.py:160
  305.0 10.8 %collective-permute-done.7 = bf16[1,64,4,1536]{3,2,1,0:T(4,128)(2,1)S(1)} collective-permute-done((bf16[1,64,4,1536]{3,2,1,0:T(4,128)(2,1)S(1)}, bf16[1,64,4,1536]{3,2,1,0:T(4,128)(2,1)S(1)}, u32[]{:S(2)}, u32[]{:S(2)}) %collective-permute-start.7) | collective-permute-done | bytes 786464 | tf_op jit(solution)/shard_map/ppermute | solution.py:38
  (123 shorter events, 36.0 us)
Async XLA Ops:
  6.5 57.0 %copy-start.2 = (bf16[1,64,4,1536]{3,2,1,0:T(4,128)(2,1)S(1)}, bf16[1,64,4,1536]{3,2,1,0:T(4,128)(2,1)}, u32[]{:S(2)}) copy-start(bf16[1,64,4,1536]{3,2,1,0:T(4,128)(2,1)} %param.16) | copy-start | bytes 2359300
  6.5 58.1 %copy-start.4 = (bf16[1,64,4,1024]{3,2,1,0:T(4,128)(2,1)S(1)}, bf16[1,64,4,1024]{3,2,1,0:T(4,128)(2,1)}, u32[]{:S(2)}) copy-start(bf16[1,64,4,1024]{3,2,1,0:T(4,128)(2,1)} %param.14) | copy-start | bytes 1572868
  6.5 14.1 %collective-permute-start = (bf16[128,1536]{1,0:T(8,128)(2,1)}, bf16[128,1536]{1,0:T(8,128)(2,1)S(1)}, u32[]{:S(2)}, u32[]{:S(2)}) collective-permute-start(bf16[128,1536]{1,0:T(8,128)(2,1)} %bitcast.124), channel_id=1, source_target_pairs={{0,1},{1,2},{2,3},{3,4},{4,5},{5,6},{6,7},{7,0},{8,9},{9,10},{10,1... | collective-permute-start | bytes 1179656 | tf_op jit(solution)/shard_map/ppermute | solution.py:27
  20.7 34.4 %copy-start.8 = (bf16[128,1536]{1,0:T(8,128)(2,1)}, bf16[128,1536]{1,0:T(8,128)(2,1)S(1)}, u32[]{:S(2)}) copy-start(bf16[128,1536]{1,0:T(8,128)(2,1)S(1)} %collective-permute-done) | copy-start | bytes 1179652
  20.7 15.9 %collective-permute-start.1 = (bf16[128,1536]{1,0:T(8,128)(2,1)S(1)}, bf16[128,1536]{1,0:T(8,128)(2,1)S(1)}, u32[]{:S(2)}, u32[]{:S(2)}) collective-permute-start(bf16[128,1536]{1,0:T(8,128)(2,1)S(1)} %collective-permute-done), channel_id=1, source_target_pairs={{0,1},{1,2},{2,3},{3,4},{4,5},{5,6},{6,7},{7,0},{8,9},{9,10},{10,1... | collective-permute-start | bytes 1179656 | tf_op jit(solution)/shard_map/ppermute | solution.py:27
  20.7 18.1 %collective-permute-start.4 = (bf16[128,1536]{1,0:T(8,128)(2,1)}, bf16[128,1536]{1,0:T(8,128)(2,1)S(1)}, u32[]{:S(2)}, u32[]{:S(2)}) collective-permute-start(bf16[128,1536]{1,0:T(8,128)(2,1)} %bitcast.125), channel_id=1, source_target_pairs={{1,0},{2,1},{3,2},{4,3},{5,4},{6,5},{7,6},{0,7},{9,8},{10,9},{11,1... | collective-permute-start | bytes 1179656 | tf_op jit(solution)/shard_map/ppermute | solution.py:29
  36.6 20.6 %copy-start.10 = (bf16[128,1536]{1,0:T(8,128)(2,1)}, bf16[128,1536]{1,0:T(8,128)(2,1)S(1)}, u32[]{:S(2)}) copy-start(bf16[128,1536]{1,0:T(8,128)(2,1)S(1)} %collective-permute-done.1) | copy-start | bytes 1179652
  36.6 18.4 %collective-permute-start.2 = (bf16[128,1536]{1,0:T(8,128)(2,1)S(1)}, bf16[128,1536]{1,0:T(8,128)(2,1)S(1)}, u32[]{:S(2)}, u32[]{:S(2)}) collective-permute-start(bf16[128,1536]{1,0:T(8,128)(2,1)S(1)} %collective-permute-done.1), channel_id=1, source_target_pairs={{0,1},{1,2},{2,3},{3,4},{4,5},{5,6},{6,7},{7,0},{8,9},{9,10},{10,1... | collective-permute-start | bytes 1179656 | tf_op jit(solution)/shard_map/ppermute | solution.py:27
  38.8 26.9 %copy-start.9 = (bf16[128,1536]{1,0:T(8,128)(2,1)}, bf16[128,1536]{1,0:T(8,128)(2,1)S(1)}, u32[]{:S(2)}) copy-start(bf16[128,1536]{1,0:T(8,128)(2,1)S(1)} %collective-permute-done.4) | copy-start | bytes 1179652
  38.8 28.0 %collective-permute-start.5 = (bf16[128,1536]{1,0:T(8,128)(2,1)S(1)}, bf16[128,1536]{1,0:T(8,128)(2,1)}, u32[]{:S(2)}, u32[]{:S(2)}) collective-permute-start(bf16[128,1536]{1,0:T(8,128)(2,1)S(1)} %collective-permute-done.4), channel_id=1, source_target_pairs={{1,0},{2,1},{3,2},{4,3},{5,4},{6,5},{7,6},{0,7},{9,8},{10,9},{11,1... | collective-permute-start | bytes 1179656 | tf_op jit(solution)/shard_map/ppermute | solution.py:29
  55.0 10.7 %copy-start.11 = (bf16[128,1536]{1,0:T(8,128)(2,1)}, bf16[128,1536]{1,0:T(8,128)(2,1)S(1)}, u32[]{:S(2)}) copy-start(bf16[128,1536]{1,0:T(8,128)(2,1)S(1)} %collective-permute-done.2) | copy-start | bytes 1179652
  55.0 15.9 %collective-permute-start.3 = (bf16[128,1536]{1,0:T(8,128)(2,1)S(1)}, bf16[128,1536]{1,0:T(8,128)(2,1)}, u32[]{:S(2)}, u32[]{:S(2)}) collective-permute-start(bf16[128,1536]{1,0:T(8,128)(2,1)S(1)} %collective-permute-done.2), channel_id=1, source_target_pairs={{0,1},{1,2},{2,3},{3,4},{4,5},{5,6},{6,7},{7,0},{8,9},{9,10},{10,1... | collective-permute-start | bytes 1179656 | tf_op jit(solution)/shard_map/ppermute | solution.py:27
  58.4 7.3 %copy-start.5 = (bf16[1,64,4,1024]{3,2,1,0:T(4,128)(2,1)S(1)}, bf16[1,64,4,1024]{3,2,1,0:T(4,128)(2,1)}, u32[]{:S(2)}) copy-start(bf16[1,64,4,1024]{3,2,1,0:T(4,128)(2,1)} %param.15) | copy-start | bytes 1572868
  59.4 15.5 %all-to-all-start = ((bf16[64,8,512]{2,0,1:T(8,128)(2,1)}), bf16[64,8,512]{2,0,1:T(8,128)(2,1)}, u32[]{:S(2)}, u32[]{:S(2)}) async-start(bf16[64,8,512]{2,0,1:T(8,128)(2,1)} %copy.40), calls=%async_computation | async-start | bytes 1048576 | tf_op jit(solution)/shard_map/all_to_all | solution.py:119
  65.7 23.4 %copy-start.7 = (bf16[1,128,1536]{2,1,0:T(8,128)(2,1)S(1)}, bf16[1,128,1536]{2,1,0:T(8,128)(2,1)}, u32[]{:S(2)}) copy-start(bf16[1,128,1536]{2,1,0:T(8,128)(2,1)} %param.17) | copy-start | bytes 1179652
  66.8 39.8 %collective-permute-start.6 = (bf16[128,1536]{1,0:T(8,128)(2,1)}, bf16[128,1536]{1,0:T(8,128)(2,1)}, u32[]{:S(2)}, u32[]{:S(2)}) collective-permute-start(bf16[128,1536]{1,0:T(8,128)(2,1)} %collective-permute-done.5), channel_id=1, source_target_pairs={{1,0},{2,1},{3,2},{4,3},{5,4},{6,5},{7,6},{0,7},{9,8},{10,9},{11,1... | collective-permute-start | bytes 1179656 | tf_op jit(solution)/shard_map/ppermute | solution.py:29
  74.8 26.6 %all-to-all-start.1 = ((bf16[64,8,512]{2,0,1:T(8,128)(2,1)}), bf16[64,8,512]{2,0,1:T(8,128)(2,1)}, u32[]{:S(2)}, u32[]{:S(2)}) async-start(bf16[64,8,512]{2,0,1:T(8,128)(2,1)} %copy.41), calls=%async_computation.1 | async-start | bytes 1048576 | tf_op jit(solution)/shard_map/all_to_all | solution.py:120
  101.5 17.5 %all-to-all-start.3 = ((bf16[64,8,512]{2,0,1:T(8,128)(2,1)}), bf16[64,8,512]{2,0,1:T(8,128)(2,1)}, u32[]{:S(2)}, u32[]{:S(2)}) async-start(bf16[64,8,512]{2,0,1:T(8,128)(2,1)} %copy.44), calls=%async_computation.3 | async-start | bytes 1048576 | tf_op jit(solution)/shard_map/all_to_all | solution.py:121
  113.2 10.7 %copy-start.13 = (s32[1,4]{1,0:T(1,128)S(1)}, s32[1,4]{1,0:T(1,128)}, u32[]{:S(2)}) copy-start(s32[1,4]{1,0:T(1,128)} %param.19) | copy-start | bytes 52
  118.9 17.5 %all-to-all-start.2 = ((bf16[64,8,512]{2,0,1:T(8,128)(2,1)}), bf16[64,8,512]{2,0,1:T(8,128)(2,1)}, u32[]{:S(2)}, u32[]{:S(2)}) async-start(bf16[64,8,512]{2,0,1:T(8,128)(2,1)} %copy.43), calls=%async_computation.2 | async-start | bytes 1048576 | tf_op jit(solution)/shard_map/all_to_all | solution.py:122
  123.1 173.3 %all-gather.3.cloned.1.call-start = ((), (), s32[]{:S(2)}) async-start(), calls=%async_computation.7 | async-start | bytes 10616832 | tf_op jit(solution)/shard_map/all_gather | solution.py:162
  185.8 7.5 %copy-start.3 = (bf16[8,512,64]{1,2,0:T(8,128)(2,1)S(1)}, bf16[8,512,64]{1,2,0:T(8,128)(2,1)}, u32[]{:S(2)}) copy-start(bf16[8,512,64]{1,2,0:T(8,128)(2,1)} %get-tuple-element.82) | copy-start | bytes 1572868
  189.1 31.1 %all-to-all-start.4 = ((bf16[8,64,512]{2,1,0:T(8,128)(2,1)}), bf16[8,64,512]{2,1,0:T(8,128)(2,1)S(1)}, u32[]{:S(2)}, u32[]{:S(2)}) async-start(bf16[8,64,512]{2,1,0:T(8,128)(2,1)} %copy.55), calls=%async_computation.4 | async-start | bytes 1048576 | tf_op jit(solution)/shard_map/all_to_all | solution.py:148
  193.9 63.6 %copy-start = (bf16[1,64,4,1536]{3,2,1,0:T(4,128)(2,1)S(1)}, bf16[1,64,4,1536]{3,2,1,0:T(4,128)(2,1)}, u32[]{:S(2)}) copy-start(bf16[1,64,4,1536]{3,2,1,0:T(4,128)(2,1)} %param.11) | copy-start | bytes 2359300
  220.2 33.2 %all-to-all-start.5 = ((bf16[8,64,512]{2,1,0:T(8,128)(2,1)}), bf16[8,64,512]{2,1,0:T(8,128)(2,1)S(1)}, u32[]{:S(2)}, u32[]{:S(2)}) async-start(bf16[8,64,512]{2,1,0:T(8,128)(2,1)} %copy.56), calls=%async_computation.5 | async-start | bytes 1048576 | tf_op jit(solution)/shard_map/all_to_all | solution.py:149
  225.5 33.4 %copy-start.12 = (f32[1,1536]{1,0:T(1,128)S(1)}, f32[1,1536]{1,0:T(1,128)}, u32[]{:S(2)}) copy-start(f32[1,1536]{1,0:T(1,128)} %param.12) | copy-start | bytes 18436
  253.3 34.1 %all-to-all-start.6 = ((bf16[8,64,512]{2,1,0:T(8,128)(2,1)}), bf16[8,64,512]{2,1,0:T(8,128)(2,1)}, u32[]{:S(2)}, u32[]{:S(2)}) async-start(bf16[8,64,512]{2,1,0:T(8,128)(2,1)} %copy.57), calls=%async_computation.6 | async-start | bytes 1048576 | tf_op jit(solution)/shard_map/all_to_all | solution.py:150
  260.2 36.3 %copy-start.6 = (bf16[256,1024]{1,0:T(8,128)(2,1)S(1)}, bf16[256,1024]{1,0:T(8,128)(2,1)}, u32[]{:S(2)}) copy-start(bf16[256,1024]{1,0:T(8,128)(2,1)} %reshape.190) | copy-start | bytes 1572868
  289.7 13.5 %copy-start.1 = (bf16[256,1536]{1,0:T(8,128)(2,1)S(1)}, bf16[256,1536]{1,0:T(8,128)(2,1)}, u32[]{:S(2)}) copy-start(bf16[256,1536]{1,0:T(8,128)(2,1)} %reshape_squeeze.2) | copy-start | bytes 2359300
  304.1 11.7 %collective-permute-start.7 = (bf16[1,64,4,1536]{3,2,1,0:T(4,128)(2,1)S(1)}, bf16[1,64,4,1536]{3,2,1,0:T(4,128)(2,1)S(1)}, u32[]{:S(2)}, u32[]{:S(2)}) collective-permute-start(bf16[1,64,4,1536]{3,2,1,0:T(4,128)(2,1)S(1)} %reshape.193), channel_id=1, source_target_pairs={{0,24},{8,0},{16,8},{24,16},{1,25},{9,1},{17,9},{25,17},{2,26},{10... | collective-permute-start | bytes 2359304 | tf_op jit(solution)/shard_map/ppermute | solution.py:38
Sparse Core Ops, SparseCore 0:
  126.1 170.3 all-gather.2
